TPU v7x, 32 devices: a whole 2x2x4 slice. The times are simulated.
32 devices in a mesh: grp: 2 (over y), seq: 4 (over z), ch: 2 (over x), sub: 2 (over core).
Axes of the slice: x: 2, y: 2, z: 4, core: 2. Of those that a mesh axis runs over, the one named last changes fastest.
Arguments:
- token_ids: int32 [2048], P(('grp', 'seq')), parts along dimension 0, may hold values from 0 to 511
- residual_in: bfloat16 [2048, 4096], P(('grp', 'seq'), ('ch', 'sub')), parts along dimension 0, may hold values from -6 to 6
- embedding: bfloat16 [512, 4096], P(None, ('ch', 'sub')), may hold values from -6 to 6
- in_weight: bfloat16 [4096, 3, 2048], P('seq', None, ('ch', 'sub')), may hold values from -0.09375 to 0.09375
- short_filter: float32 [3, 3, 2048], P(None, None, ('ch', 'sub')), may hold values from -3 to 3
- decay_rate: float32 [16, 2048], P(None, ('ch', 'sub')), may hold values from 1e-05 to 0.05
- residue: float32 [16, 2048], P(None, ('ch', 'sub')), may hold values from -0.24 to 0.24
- skip: float32 [2048], P(('ch', 'sub')), may hold values from -4 to 4
Outputs:
- mixed_out: bfloat16 [2048, 2048], P(('grp', 'seq'), ('ch', 'sub')), parts along dimension 0
There are 2 independent parts, one for each index of `grp`. A program takes and returns all parts, laid end to end along the dimension named above; an argument that names none is the same for every part. Nothing has to cross between parts.
All inputs are finite; a program needn't handle non-finite values.
Results may differ from a plain program's by a relative error of at most 0.0095.
Values may be sent and summed in bfloat16 or wider, within the bound.
A program may use at most 64 MiB of HBM per device.

v0:
```python
import jax
import jax.numpy as jnp
from jax import lax
from jax.sharding import PartitionSpec as P

PRECISE = lax.Precision.HIGHEST
TWO_PI = 6.283185307179586


def shifted(x, axis, by):
    peers = lax.axis_size(axis)
    pairs = [(i, i + by) for i in range(peers) if 0 <= i + by < peers]
    return lax.ppermute(x, axis, pairs)


def swapped(value, axis, apart):
    mask = 2**apart
    pairs = [(source, source ^ mask) for source in range(lax.axis_size(axis))]
    return lax.ppermute(value, axis, pairs)


def reversed_bits(number, bit_count):
    result = jnp.zeros_like(number)
    for section_bit in range(bit_count):
        result = result + (number >> section_bit & 1) * (1 << bit_count - 1 - section_bit)
    return result


def angle_table(left_idx, right_idx, period):
    wrapped = left_idx[:, None] * right_idx[None, :] % period
    return TWO_PI * wrapped.astype(jnp.float32) / period


def complex_mix(mat_re, mat_im, data_re, data_im):
    real_part = jnp.einsum("kr,rjc->kjc", mat_re, data_re, precision=PRECISE) - jnp.einsum(
        "kr,rjc->kjc", mat_im, data_im, precision=PRECISE
    )
    imag_part = jnp.einsum("kr,rjc->kjc", mat_re, data_im, precision=PRECISE) + jnp.einsum(
        "kr,rjc->kjc", mat_im, data_re, precision=PRECISE
    )
    return (real_part, imag_part)


def complex_dot(mat_re, mat_im, data_re, data_im):
    real_part = jnp.dot(mat_re, data_re, precision=PRECISE) - jnp.dot(
        mat_im, data_im, precision=PRECISE
    )
    imag_part = jnp.dot(mat_re, data_im, precision=PRECISE) + jnp.dot(
        mat_im, data_re, precision=PRECISE
    )
    return (real_part, imag_part)


def shards(token_ids, residual_in, embedding, in_weight, short_filter, decay_rate, residue, skip):
    tok_rows = residual_in.shape[0]
    vocab_size = embedding.shape[0]
    channels = skip.shape[0]
    seq_parts = lax.axis_size("seq")
    bit_count = seq_parts.bit_length() - 1
    my_index = lax.axis_index("seq")
    length = tok_rows * seq_parts
    padded_len = 2 * length
    group_rows = tok_rows // seq_parts
    onehot = (token_ids[:, None] == jnp.arange(vocab_size, dtype=jnp.int32)[None, :]).astype(
        jnp.bfloat16
    )
    embedded = jnp.dot(onehot, embedding, preferred_element_type=jnp.float32)
    inputs = (residual_in.astype(jnp.float32) + embedded).astype(jnp.bfloat16)
    features = lax.all_gather(inputs, ("ch", "sub"), axis=1, tiled=True)
    piece_rows = lax.all_gather(in_weight, "seq", axis=0, tiled=True)
    flat_piece = piece_rows.reshape(piece_rows.shape[0], 3 * channels)
    projected = jnp.dot(features, flat_piece, preferred_element_type=jnp.float32)
    projected = projected.astype(jnp.bfloat16).reshape(tok_rows, 3, channels)
    rim_rows = shifted(projected[tok_rows - 2 :], "seq", 1)
    extended = jnp.concatenate([rim_rows, projected], axis=0).astype(jnp.float32)
    mixed_in = (
        short_filter[0] * extended[2:]
        + short_filter[1] * extended[1:-1]
        + short_filter[2] * extended[:-2]
    )
    query_gate = mixed_in[:, 0]
    product = (mixed_in[:, 1] * mixed_in[:, 2]).astype(jnp.bfloat16)
    local_pos = jnp.arange(tok_rows, dtype=jnp.int32)
    sources = jnp.arange(seq_parts, dtype=jnp.int32)
    within_rows = my_index * group_rows + jnp.arange(group_rows, dtype=jnp.int32)
    block_pos = sources[:, None] * tok_rows + within_rows[None, :]
    block_angle = TWO_PI * block_pos.astype(jnp.float32) / padded_len
    pos_angle = TWO_PI * (my_index * tok_rows + local_pos).astype(jnp.float32) / padded_len
    values = product.astype(jnp.float32)
    state_re = jnp.concatenate([values, values * jnp.cos(pos_angle)[:, None]], -1)
    state_im = jnp.concatenate([jnp.zeros_like(values), -values * jnp.sin(pos_angle)[:, None]], -1)
    state_now = jnp.stack([state_re, state_im])
    for section_bit in range(bit_count - 1, -1, -1):
        half_span = 1 << section_bit
        partner = swapped(state_now.astype(jnp.bfloat16), "seq", section_bit).astype(
            state_now.dtype
        )
        upper_half = my_index >> section_bit & 1 == 1
        phase_now = TWO_PI * (my_index % half_span).astype(jnp.float32) / (2 * half_span)
        difference = partner - state_now
        rot_re = difference[0] * jnp.cos(phase_now) + difference[1] * jnp.sin(phase_now)
        rot_im = difference[1] * jnp.cos(phase_now) - difference[0] * jnp.sin(phase_now)
        state_now = jnp.where(upper_half, jnp.stack([rot_re, rot_im]), state_now + partner)
    own_freq = reversed_bits(my_index, bit_count)
    holders = reversed_bits(sources, bit_count)
    twist_angle = TWO_PI * (local_pos * own_freq % length).astype(jnp.float32) / length
    twist_re = jnp.cos(twist_angle)[:, None]
    twist_im = -jnp.sin(twist_angle)[:, None]
    spec_re = state_now[0] * twist_re - state_now[1] * twist_im
    spec_im = state_now[0] * twist_im + state_now[1] * twist_re
    kernel_table = angle_table(local_pos, local_pos, tok_rows)
    dft_re = jnp.cos(kernel_table)
    dft_im = -jnp.sin(kernel_table)
    spec_re, spec_im = complex_dot(dft_re, dft_im, spec_re, spec_im)
    parity = (jnp.arange(2 * channels, dtype=jnp.int32) >= channels).astype(jnp.int32)
    full_freq = 2 * (own_freq + seq_parts * local_pos)[:, None] + parity[None, :]
    freq_angle = TWO_PI * full_freq.astype(jnp.float32) / padded_len
    half_sine = jnp.sin(0.5 * freq_angle)
    sine_full = jnp.sin(freq_angle)
    sign_flip = 1.0 - 2.0 * parity.astype(jnp.float32)
    rates_both = jnp.concatenate([decay_rate, decay_rate], -1)
    residues_both = jnp.concatenate([residue, residue], -1)
    filt_re = jnp.zeros_like(spec_re)
    filt_im = jnp.zeros_like(spec_re)
    for mode_index in range(rates_both.shape[0]):
        rate_now = rates_both[mode_index]
        decay_now = jnp.exp(-rate_now)
        numerator = residues_both[mode_index] * (1.0 - sign_flip * jnp.exp(-rate_now * length))
        denom_re = -jnp.expm1(-rate_now) + 2.0 * decay_now * half_sine * half_sine
        denom_im = decay_now * sine_full
        scaled = numerator / (denom_re * denom_re + denom_im * denom_im)
        filt_re = filt_re + scaled * denom_re
        filt_im = filt_im - scaled * denom_im
    prod_re = spec_re * filt_re - spec_im * filt_im
    prod_im = spec_re * filt_im + spec_im * filt_re
    inv_re, inv_im = complex_dot(dft_re, -dft_im, prod_re, prod_im)
    back_re = inv_re * twist_re + inv_im * twist_im
    back_im = inv_im * twist_re - inv_re * twist_im
    returned = lax.all_to_all(
        jnp.stack([back_re, back_im]).reshape(2, 1, tok_rows, 2 * channels).astype(jnp.bfloat16),
        "seq",
        split_axis=2,
        concat_axis=1,
        tiled=True,
    ).astype(jnp.float32)
    inverse_angle = angle_table(sources, holders, seq_parts)
    block_re, block_im = complex_mix(
        jnp.cos(inverse_angle), jnp.sin(inverse_angle), returned[0], returned[1]
    )
    conv_blocks = (
        block_re[..., :channels]
        + jnp.cos(block_angle)[:, :, None] * block_re[..., channels:]
        - jnp.sin(block_angle)[:, :, None] * block_im[..., channels:]
    )
    conv_blocks = conv_blocks / padded_len
    conv_rows = lax.all_to_all(conv_blocks, "seq", split_axis=0, concat_axis=1, tiled=True)[0]
    mixed_out = (query_gate * (conv_rows + skip * product.astype(jnp.float32))).astype(jnp.bfloat16)
    return mixed_out


def solution(mesh):
    return jax.shard_map(
        shards,
        mesh=mesh,
        in_specs=(
            P(("grp", "seq")),
            P(("grp", "seq"), ("ch", "sub")),
            P(None, ("ch", "sub")),
            P("seq", None, ("ch", "sub")),
            P(None, None, ("ch", "sub")),
            P(None, ("ch", "sub")),
            P(None, ("ch", "sub")),
            P(("ch", "sub")),
        ),
        out_specs=P(("grp", "seq"), ("ch", "sub")),
        check_vma=False,
    )
```

profile of v0, /device:TPU:2, one launch (start us, length us, event | category | flops | bytes accessed | tf_op | source)
XLA Modules:
  0.0 443.3 jit_solution(15915545846270894361)
XLA Ops:
  6.5 1.2 copy-done
  7.8 2.3 fusion.5
  10.2 4.7 %copy.55 = bf16[1024,3,512]{0,2,1:T(8,128)(2,1)} copy(bf16[1024,3,512]{2,0,1:T(8,128)(2,1)} %param.11) | data formatting | bytes 6291456 | tf_op args[3]
  14.9 0.7 copy-done.6
  15.6 17.3 %all-gather.3.cloned.1.call-done = bf16[256,4096]{1,0:T(8,128)(2,1)} async-done(((bf16[256,1024]{1,0:T(8,128)(2,1)}), bf16[256,4096]{1,0:T(8,128)(2,1)}) %all-gather.3.cloned.1.call-update) | async-done | bytes 2097168 | tf_op jit(solution)/shard_map/all_gather | solution.py:69
  33.0 220.9 %all-gather.5.cloned.1.call-done = bf16[4096,3,512]{0,2,1:T(8,128)(2,1)} async-done(((bf16[1024,3,512]{0,2,1:T(8,128)(2,1)}), bf16[4096,3,512]{0,2,1:T(8,128)(2,1)}) %all-gather.5.cloned.1.call-update) | async-done | bytes 12582928 | tf_op jit(solution)/shard_map/all_gather | solution.py:70
  253.9 8.7 %convolution_convert_fusion = bf16[256,1536]{1,0:T(8,128)(2,1)S(1)} fusion(bf16[256,4096]{1,0:T(8,128)(2,1)} %all-gather.3.cloned.1.call-done, bf16[4096,1536]{0,1:T(8,128)(2,1)} %bitcast.208), kind=kOutput, calls=%fused_computation.4 | convolution fusion | flops 3221618688 | bytes 15466496 | tf_op jit(solution)/shard_map/dot_general | solution.py:72
  262.5 1.8 collective-permute-start
  264.3 0.3 copy.57
  264.6 0.3 copy.58
  264.9 0.3 collective-permute-done
  265.2 0.2 maximum_convert_fusion
  265.4 0.5 fusion.2
  266.3 0.8 copy-done.3
  267.2 1.3 fusion.4
  268.4 3.5 collective-permute-start.1
  272.2 0.8 constant_dynamic-update-slice_fusion.3
  272.9 0.8 constant_dynamic-update-slice_fusion
  273.7 0.6 fusion.155
  274.4 42.5 %collective-permute-done.1 = bf16[2,256,1024]{2,1,0:T(8,128)(2,1)S(1)} collective-permute-done((bf16[2,256,1024]{2,1,0:T(8,128)(2,1)}, bf16[2,256,1024]{2,1,0:T(8,128)(2,1)S(1)}, u32[]{:S(2)}, u32[]{:S(2)}) %collective-permute-start.1) | collective-permute-done | bytes 1048608 | tf_op jit(solution)/shard_map/ppermute | solution.py:19
  316.8 0.3 convert_subtract_fusion.1
  317.2 0.6 copy-done.4
  317.8 0.3 multiply_add_fusion.4
  318.1 3.2 fusion.171
  321.3 0.6 add_multiply_fusion
  322.3 23.2 %collective-permute-done.2 = bf16[2,256,1024]{2,1,0:T(8,128)(2,1)S(1)} collective-permute-done((bf16[2,256,1024]{2,1,0:T(8,128)(2,1)}, bf16[2,256,1024]{2,1,0:T(8,128)(2,1)S(1)}, u32[]{:S(2)}, u32[]{:S(2)}) %collective-permute-start.2) | collective-permute-done | bytes 1048608 | tf_op jit(solution)/shard_map/ppermute | solution.py:19
  345.5 0.3 convert_subtract_fusion
  346.0 0.6 fusion.1
  346.6 2.2 fusion.72
  348.8 2.2 fusion.70
  351.1 2.2 convolution_subtract_fusion.2
  353.3 17.8 %multiply_add_fusion = (f32[256,1024]{1,0:T(8,128)S(1)}, f32[256,1024]{1,0:T(8,128)S(1)}, f32[256,1024]{1,0:T(8,128)S(1)}, f32[256,1024]{1,0:T(8,128)S(1)}) fusion(f32[256,1024]{1,0:T(8,128)S(1)} %convolution_subtract_fusion.2, f32[1024]{0:T(1024)S(1)} %bitcast.145, f32[1024]{0:T(1024)S(1)} %bitcast.146, f32[1024]{0:T(1024)S(1)} %bitcast.191, ...), kind=kOutput, calls=%fused_computation.59 | convolution fusion | flops 859242496 | bytes 8657920 | tf_op jit(solution)/shard_map/dot_general | solution.py:48
  371.2 2.0 fusion.66
  373.2 0.5 multiply_subtract_fusion
  373.7 2.0 fusion.68
  375.7 2.3 convolution_add_fusion.1
  378.0 2.3 fusion.38
  380.4 2.1 copy.59
  382.5 4.1 all-to-all-start
  387.0 24.0 %all-to-all-done = bf16[2,1,256,1024]{3,0,1,2:T(2,128)(2,1)S(1)} async-done(((bf16[2,1,256,1024]{3,0,1,2:T(2,128)(2,1)}), bf16[2,1,256,1024]{3,0,1,2:T(2,128)(2,1)S(1)}, u32[]{:S(2)}, u32[]{:S(2)}) %all-to-all-start) | async-done | bytes 1048608 | tf_op jit(solution)/shard_map/all_to_all | solution.py:139
  411.0 1.5 fusion.175
  412.7 1.1 fusion.52
  413.7 1.1 fusion.50
  415.0 1.1 fusion.47
  416.1 1.1 convolution_subtract_fusion
  417.2 0.3 fusion.42
  417.7 16.5 %all_to_all.8 = f32[4,64,512]{2,1,0:T(8,128)S(1)} all-to-all(f32[4,64,512]{2,1,0:T(8,128)S(1)} %copy.68), channel_id=1, replica_groups=mesh['grp'=2,'seq'=4,'ch'=2,'sub'=2] {'seq'}, dimensions={0} | all-to-all | bytes 1048576 | tf_op jit(solution)/shard_map/all_to_all | solution.py:156
  434.2 1.8 fusion.46
  (58 shorter events, 2.2 us)
Async XLA Ops:
  6.5 1.2 copy-start
  6.5 26.4 %all-gather.3.cloned.1.call-start = ((), (), s32[]{:S(2)}) async-start(), calls=%async_computation.2 | async-start | bytes 2621440 | tf_op jit(solution)/shard_map/all_gather | solution.py:69
  10.1 243.7 %all-gather.5.cloned.1.call-start = ((), (), s32[]{:S(2)}) async-start(), calls=%async_computation.3 | async-start | bytes 15728640 | tf_op jit(solution)/shard_map/all_gather | solution.py:70
  14.9 0.7 copy-start.6
  262.5 2.6 collective-permute-start
  265.9 1.2 copy-start.3
  267.1 50.0 %copy-start.2 = (f32[1,256,1024]{2,1,0:T(8,128)}, f32[1,256,1024]{2,1,0:T(8,128)S(1)}, u32[]{:S(2)}) copy-start(f32[1,256,1024]{2,1,0:T(8,128)S(1)} %maximum_bitcast_fusion) | copy-start | bytes 3145732
  267.2 5.0 %copy-start.5 = (f32[16,512]{1,0:T(8,128)S(1)}, f32[16,512]{1,0:T(8,128)}, u32[]{:S(2)}) copy-start(f32[16,512]{1,0:T(8,128)} %param.14) | copy-start | bytes 98308
  268.4 48.4 %collective-permute-start.1 = (bf16[2,256,1024]{2,1,0:T(8,128)(2,1)}, bf16[2,256,1024]{2,1,0:T(8,128)(2,1)S(1)}, u32[]{:S(2)}, u32[]{:S(2)}) collective-permute-start(bf16[2,256,1024]{2,1,0:T(8,128)(2,1)} %fusion.4), channel_id=1, source_target_pairs={{0,8},{4,12},{8,0},{12,4},{1,9},{5,13},{9,1},{13,5},{2,10},{6,14},... | collective-permute-start | bytes 3145736 | tf_op jit(solution)/shard_map/ppermute | solution.py:19
  316.8 1.0 copy-start.4
  321.3 24.2 %collective-permute-start.2 = (bf16[2,256,1024]{2,1,0:T(8,128)(2,1)}, bf16[2,256,1024]{2,1,0:T(8,128)(2,1)S(1)}, u32[]{:S(2)}, u32[]{:S(2)}) collective-permute-start(bf16[2,256,1024]{2,1,0:T(8,128)(2,1)} %get-tuple-element.8), channel_id=1, source_target_pairs={{0,4},{4,0},{8,12},{12,8},{1,5},{5,1},{9,13},{13,9},{2,6},{6,2},{1... | collective-permute-start | bytes 3145736 | tf_op jit(solution)/shard_map/ppermute | solution.py:19
  351.0 2.3 copy-start.7
  351.0 2.3 copy-start.8
  351.0 2.3 copy-start.9
  351.0 2.3 copy-start.10
  351.0 2.3 copy-start.11
  351.0 2.3 copy-start.12
  351.0 2.3 copy-start.13
  351.0 2.3 copy-start.15
  382.5 28.5 %all-to-all-start = ((bf16[2,1,256,1024]{3,0,1,2:T(2,128)(2,1)}), bf16[2,1,256,1024]{3,0,1,2:T(2,128)(2,1)S(1)}, u32[]{:S(2)}, u32[]{:S(2)}) async-start(bf16[2,1,256,1024]{3,0,1,2:T(2,128)(2,1)} %copy.59), calls=%async_computation | async-start | bytes 2097152 | tf_op jit(solution)/shard_map/all_to_all | solution.py:139
  417.2 17.0 %copy-start.14 = (f32[512]{0:T(512)S(1)}, f32[512]{0:T(512)}, u32[]{:S(2)}) copy-start(f32[512]{0:T(512)} %param.15) | copy-start | bytes 6148
  417.2 18.8 %copy-start.1 = (bf16[512,1024]{1,0:T(8,128)(2,1)S(1)}, bf16[512,1024]{1,0:T(8,128)(2,1)}, u32[]{:S(2)}) copy-start(bf16[512,1024]{1,0:T(8,128)(2,1)} %param.10) | copy-start | bytes 3145732
Sparse Core Ops, SparseCore 0:
  10.3 22.6 all-gather.2
  34.5 219.2 all-gather.4
where the time goes:
time: 448 us; the launch traced here: 443 us
  waiting for transfers between devices  328 us (73%)
  matrix products  48.4 us (11%)
  blocking collectives  16.5 us (4%)
  local copies, waits for them, and re-layouts  14.6 us (3%)
  between operations  14.5 us (3%)
  other arithmetic  11.7 us (3%)
  starting transfers between devices  9.46 us (2%)
    all_gather x1, waiting for transfers between devices, shards(): piece_rows = lax.all_gather(in_weight, 'seq', axis=0, tiled=True)  221 us
    ppermute x2, waiting for transfers between devices, swapped(): return lax.ppermute(value, axis, pairs)  65.7 us
    all_to_all x1, waiting for transfers between devices, shards(): lax.all_to_all(jnp.stack([back_re, back_im]).reshape(2, 1, tok_rows, 2 *...  24 us
    dot_general x2, matrix products, complex_dot(): jnp.dot(mat_im, data_re, precision=PRECISE)  20.1 us
    all_gather x1, waiting for transfers between devices, shards(): features = lax.all_gather(inputs, ('ch', 'sub'), axis=1, tiled=True)  17.3 us
    all_to_all x1, blocking collectives, shards(): lax.all_to_all(conv_blocks, 'seq', split_axis=0, concat_axis=1, tiled=True)  16.5 us
    unnamed x37, local copies, waits for them, and re-layouts  9.23 us
  transfers between devices with their start and end apart: 6, of which 6 were waited for; matrix products, arithmetic and copies ran while one was open for 2% of the time, Pallas kernels for 0%

commit v1 on v0

--- a/solution.py
+++ b/solution.py
@@ -1,6 +1,10 @@
+import functools
+
 import jax
 import jax.numpy as jnp
 from jax import lax
+from jax.experimental import pallas as pl
+from jax.experimental.pallas import tpu as pltpu
 from jax.sharding import PartitionSpec as P
 
 PRECISE = lax.Precision.HIGHEST
@@ -158,9 +162,125 @@
     return mixed_out
 
 
+def mix_and_scan(rows, modes, part_ref, taps_ref, rate_ref, residue_ref, skip_ref, out_ref, proj, values, gate, result):
+    total, lanes = out_ref.shape
+    lead = proj.shape[1] - total
+    taps_count = taps_ref.shape[0]
+    span = total // rows
+    for g in range(3):
+        proj[g, :lead, :] = jnp.zeros((lead, lanes), jnp.float32)
+    parts = part_ref.shape[0]
+
+    @pl.loop(0, 3)
+    def _(g):
+        acc = part_ref[0, g].astype(jnp.float32)
+        for i in range(1, parts):
+            acc = acc + part_ref[i, g].astype(jnp.float32)
+        proj[g, lead:, :] = acc.astype(jnp.bfloat16).astype(jnp.float32)
+
+    mixed = []
+    for g in range(3):
+        acc = None
+        for i in range(taps_count):
+            term = taps_ref[i, g : g + 1, :] * proj[g, pl.ds(lead - i, total), :]
+            acc = term if acc is None else acc + term
+        if g == 0:
+            gate[...] = acc
+        else:
+            mixed.append(acc)
+    values[...] = (mixed[0] * mixed[1]).astype(jnp.bfloat16).astype(jnp.float32)
+
+    decay = [jnp.broadcast_to(jnp.exp(-rate_ref[m : m + 1, :]), (rows, lanes)) for m in range(modes)]
+    zero = jnp.zeros((rows, lanes), jnp.float32)
+
+    def ends(j, state):
+        now = values[pl.ds(j, rows, stride=span), :]
+        return tuple(u * d + now for u, d in zip(state, decay))
+
+    state = lax.fori_loop(0, span, ends, (zero,) * modes, unroll=4)
+    index = lax.broadcasted_iota(jnp.int32, (rows, lanes), 0)
+
+    def down(x, by):
+        return jnp.where(index >= by, pltpu.roll(x, by, 0), 0.0)
+
+    entering = []
+    for m in range(modes):
+        carry = down(state[m], 1)
+        by = 1
+        while by < rows:
+            carry = carry + jnp.exp(-rate_ref[m : m + 1, :] * (span * by)) * down(carry, by)
+            by *= 2
+        entering.append(carry)
+    weight = [jnp.broadcast_to(residue_ref[m : m + 1, :], (rows, lanes)) for m in range(modes)]
+    direct = jnp.broadcast_to(skip_ref[...], (rows, lanes))
+
+    def scan(j, state):
+        at = pl.ds(j, rows, stride=span)
+        now = values[at, :]
+        state = tuple(u * d + now for u, d in zip(state, decay))
+        terms = [u * w for u, w in zip(state, weight)] + [direct * now]
+        while len(terms) > 1:
+            terms = [a + b for a, b in zip(terms[::2], terms[1::2])] + terms[len(terms) // 2 * 2 :]
+        result[at, :] = gate[at, :] * terms[0]
+        return state
+
+    lax.fori_loop(0, span, scan, tuple(entering), unroll=4)
+    out_ref[...] = result[...].astype(out_ref.dtype)
+
+
+def convolved(partial, short_filter, decay_rate, residue, skip):
+    parts, _, total, lanes = partial.shape
+    modes = decay_rate.shape[0]
+    rows = 8
+    f32 = jnp.float32
+    return pl.pallas_call(
+        functools.partial(mix_and_scan, rows, modes),
+        out_shape=jax.ShapeDtypeStruct((total, lanes), jnp.bfloat16),
+        in_specs=[pl.BlockSpec(memory_space=pltpu.VMEM)] * 5,
+        out_specs=pl.BlockSpec(memory_space=pltpu.VMEM),
+        scratch_shapes=[
+            pltpu.VMEM((3, total + 8, lanes), f32),
+            pltpu.VMEM((total, lanes), f32),
+            pltpu.VMEM((total, lanes), f32),
+            pltpu.VMEM((total, lanes), f32),
+        ],
+        compiler_params=pltpu.CompilerParams(vmem_limit_bytes=40 * 2**20),
+    )(partial, short_filter, decay_rate, residue, skip.reshape(1, lanes))
+
+
+def fast_shards(token_ids, residual_in, embedding, in_weight, short_filter, decay_rate, residue, skip):
+    tok_rows, width = residual_in.shape
+    vocab_size = embedding.shape[0]
+    channels = skip.shape[0]
+    seq_parts = lax.axis_size("seq")
+    me = lax.axis_index("seq")
+    lanes = channels // seq_parts
+    total = tok_rows * seq_parts
+    onehot = (token_ids[:, None] == jnp.arange(vocab_size, dtype=jnp.int32)[None, :]).astype(jnp.bfloat16)
+    embedded = jnp.dot(onehot, embedding, preferred_element_type=jnp.float32)
+    inputs = (residual_in.astype(jnp.float32) + embedded).astype(jnp.bfloat16)
+    pairs = [(i * seq_parts + j, j * seq_parts + i) for i in range(seq_parts) for j in range(seq_parts)]
+    turned = lax.ppermute(inputs, ("seq", "ch", "sub"), pairs)
+    rows_all = lax.all_gather(turned, ("ch", "sub"), axis=0, tiled=True)
+    weight = in_weight.transpose(1, 0, 2).reshape(3, width, seq_parts, lanes)
+    partial = jnp.einsum("td,gdsc->sgtc", rows_all, weight, preferred_element_type=jnp.float32).astype(jnp.bfloat16)
+    partial = lax.all_to_all(partial, "seq", split_axis=0, concat_axis=0, tiled=True)
+
+    def own(x):
+        return lax.dynamic_slice_in_dim(x, me * lanes, lanes, axis=x.ndim - 1)
+
+    mixed = convolved(partial, own(short_filter), own(decay_rate), own(residue), own(skip))
+    return lax.all_to_all(mixed, "seq", split_axis=0, concat_axis=1, tiled=True)
+
+
+def fits(mesh):
+    seq_parts = mesh.shape["seq"]
+    return seq_parts == mesh.shape["ch"] * mesh.shape["sub"]
+
+
 def solution(mesh):
     return jax.shard_map(
-        shards,
+        fast_shards if fits(mesh) else shards,
         mesh=mesh,
         in_specs=(
             P(("grp", "seq")),

time: 448 us -> 168 us (0.38)
  waiting for transfers between devices: 328 us -> 114 us
  matrix products: 48.4 us -> 8.36 us
  other arithmetic: 11.7 us -> 0 us
  local copies, waits for them, and re-layouts: 14.6 us -> 2.9 us
  Pallas kernels: 0 us -> 5.7 us
  blocking collectives: 16.5 us -> 10.9 us
    all_gather x2 -> x1, waiting for transfers between devices: 238 us -> 20.2 us  [fast_shards(): rows_all = lax.all_gather(turned, ('ch', 'sub'), axis=0, tiled=True)]
    all_to_all x1, waiting for transfers between devices: 24 us -> 69.1 us  [fast_shards(): lax.all_to_all(partial, 'seq', split_axis=0, concat_axis=0, tiled=True)]
    ppermute x3 -> x1, waiting for transfers between devices: 65.9 us -> 24.9 us  [fast_shards(): turned = lax.ppermute(inputs, ('seq', 'ch', 'sub'), pairs)]
    dot_general x14 -> x2, matrix products: 48.4 us -> 8.36 us  [the longest x1 6.36 us: fast_shards(): jnp.einsum('td,gdsc->sgtc', rows_all, weight, preferred_element_type=jnp....]
    unnamed x37 -> x2, local copies, waits for them, and re-layouts: 9.23 us -> 0.01 us
    convert_element_type x6 -> x0, other arithmetic: 6.59 us -> none  [the longest x2 4.42 us: shards(): state_now.astype(jnp.bfloat16)]
    pallas_call x0 -> x1, Pallas kernels: none -> 5.7 us  [convolved(): pl.pallas_call(functools.partial(mix_and_scan, rows, modes), out_shape=ja...]
    all_to_all x1, blocking collectives: 16.5 us -> 10.9 us  [fast_shards(): return lax.all_to_all(mixed, 'seq', split_axis=0, concat_axis=1, tiled=True)]
  transfers between devices with their start and end apart: 6 -> 3, of which waited for: 6 -> 3; matrix products, arithmetic and copies ran while one was open for 2% -> 1% of each run, Pallas kernels for 0% -> 0%
where the time goes in v1:
time: 168 us; the launch traced here: 165 us
  waiting for transfers between devices  114 us (68%)
  between operations  13.4 us (8%)
  blocking collectives  10.9 us (6%)
  starting transfers between devices  9.28 us (6%)
  matrix products  8.36 us (5%)
  Pallas kernels  5.7 us (3%)
  local copies, waits for them, and re-layouts  2.9 us (2%)
    all_to_all x1, waiting for transfers between devices, fast_shards(): lax.all_to_all(partial, 'seq', split_axis=0, concat_axis=0, tiled=True)  69.1 us
    ppermute x1, waiting for transfers between devices, fast_shards(): turned = lax.ppermute(inputs, ('seq', 'ch', 'sub'), pairs)  24.9 us
    all_gather x1, waiting for transfers between devices, fast_shards(): rows_all = lax.all_gather(turned, ('ch', 'sub'), axis=0, tiled=True)  20.2 us
    all_to_all x1, blocking collectives, fast_shards(): return lax.all_to_all(mixed, 'seq', split_axis=0, concat_axis=1, tiled=True)  10.9 us
    dot_general x1, matrix products, fast_shards(): jnp.einsum('td,gdsc->sgtc', rows_all, weight, preferred_element_type=jnp....  6.36 us
    pallas_call x1, Pallas kernels, convolved(): pl.pallas_call(functools.partial(mix_and_scan, rows, modes), out_shape=ja...  5.7 us
    all_to_all x1, starting transfers between devices, fast_shards(): lax.all_to_all(partial, 'seq', split_axis=0, concat_axis=0, tiled=True)  4.81 us
    ppermute x1, starting transfers between devices, fast_shards(): turned = lax.ppermute(inputs, ('seq', 'ch', 'sub'), pairs)  4.47 us
  transfers between devices with their start and end apart: 3, of which 3 were waited for; matrix products, arithmetic and copies ran while one was open for 1% of the time, Pallas kernels for 0%

profile of v1, /device:TPU:2, one launch (start us, length us, event | category | flops | bytes accessed | tf_op | source)
XLA Modules:
  0.0 164.8 jit_solution(7426061112052375483)
XLA Ops:
  6.5 0.0 copy-start
  6.5 0.0 all-gather.2.cloned.1.call-start
  6.5 2.0 %fusion.6 = bf16[256,1024]{1,0:T(8,128)(2,1)S(1)} fusion(bf16[512,1024]{1,0:T(8,128)(2,1)} %param.10, bf16[256,1024]{1,0:T(8,128)(2,1)} %param.9, s32[256]{0:T(256)} %param.8), kind=kOutput, calls=%fused_computation.6 | convolution fusion | flops 269352960 | bytes 2098176 | tf_op jit(solution)/shard_map/dot_general | solution.py:260
  8.5 4.5 %collective-permute-start = (bf16[256,1024]{1,0:T(8,128)(2,1)S(1)}, bf16[256,1024]{1,0:T(8,128)(2,1)}, u32[]{:S(2)}, u32[]{:S(2)}) collective-permute-start(bf16[256,1024]{1,0:T(8,128)(2,1)S(1)} %fusion.6), channel_id=1, source_target_pairs={{0,0},{1,4},{2,8},{3,12},{4,1},{5,5},{6,9},{7,13},{8,2},{9,6},{10,... | collective-permute-start | bytes 1572872 | tf_op jit(solution)/shard_map/ppermute | solution.py:263
  13.0 24.9 %collective-permute-done = bf16[256,1024]{1,0:T(8,128)(2,1)} collective-permute-done((bf16[256,1024]{1,0:T(8,128)(2,1)S(1)}, bf16[256,1024]{1,0:T(8,128)(2,1)}, u32[]{:S(2)}, u32[]{:S(2)}) %collective-permute-start) | collective-permute-done | bytes 524320 | tf_op jit(solution)/shard_map/ppermute | solution.py:263
  37.9 0.0 all-gather.2.cloned.1.call-update
  37.9 20.2 %all-gather.2.cloned.1.call-done = bf16[1024,1024]{1,0:T(8,128)(2,1)} async-done(((bf16[256,1024]{1,0:T(8,128)(2,1)}), bf16[1024,1024]{1,0:T(8,128)(2,1)}) %all-gather.2.cloned.1.call-update) | async-done | bytes 2097168 | tf_op jit(solution)/shard_map/all_gather | solution.py:264
  58.2 0.0 copy-done
  58.2 6.4 %convert_bitcast_fusion = bf16[4,3,1024,128]{3,2,1,0:T(8,128)(2,1)} fusion(bf16[1024,1024]{1,0:T(8,128)(2,1)} %all-gather.2.cloned.1.call-done, bf16[1024,3,512]{2,0,1:T(8,128)(2,1)S(1)} %copy-done), kind=kOutput, calls=%fused_computation.3 | convolution fusion | flops 3222798336 | bytes 8388608 | tf_op jit(solution)/shard_map/td,gdsc->sgtc/dot_general | solution.py:266
  64.6 4.8 %all-to-all-start = ((bf16[4,3,1024,128]{3,2,1,0:T(8,128)(2,1)}), bf16[4,3,1024,128]{3,2,1,0:T(8,128)(2,1)}, u32[]{:S(2)}, u32[]{:S(2)}) async-start(bf16[4,3,1024,128]{3,2,1,0:T(8,128)(2,1)} %convert_bitcast_fusion), calls=%async_computation | async-start | bytes 6291456 | tf_op jit(solution)/shard_map/all_to_all | solution.py:267
  69.4 0.8 dynamic-slice_bitcast_fusion.skip_ref
  70.1 0.7 constant_dynamic-slice_fusion.2.taps_ref
  70.8 0.7 constant_dynamic-slice_fusion
  71.5 69.1 %all-to-all-done.part_ref = bf16[4,3,1024,128]{3,2,1,0:T(8,128)(2,1)} async-done(((bf16[4,3,1024,128]{3,2,1,0:T(8,128)(2,1)}), bf16[4,3,1024,128]{3,2,1,0:T(8,128)(2,1)}, u32[]{:S(2)}, u32[]{:S(2)}) %all-to-all-start) | async-done | bytes 3145760 | tf_op jit(solution)/shard_map/all_to_all | solution.py:267
  140.6 5.7 %shard_map.82 = bf16[1024,128]{1,0:T(8,128)(2,1)S(1)} custom-call(bf16[4,3,1024,128]{3,2,1,0:T(8,128)(2,1)} %all-to-all-done.part_ref, f32[3,3,128]{2,1,0:T(4,128)S(1)} %constant_dynamic-slice_fusion.2.taps_ref, f32[16,128]{1,0:T(8,128)S(1)} %get-tuple-element.6.rate_ref, f32[16,128]{1,0:T(8,128)S(1)} %get-tuple-element.5.residue_ref, ...), custom_call_target="tpu_custom_call" | custom-call | tf_op jit(solution)/shard_map/pallas_call | solution.py:236
  146.3 10.9 %all_to_all.24 = bf16[4,256,128]{2,1,0:T(8,128)(2,1)S(1)} all-to-all(bf16[4,256,128]{2,1,0:T(8,128)(2,1)S(1)} %bitcast.25), channel_id=1, replica_groups=mesh['grp'=2,'seq'=4,'ch'=2,'sub'=2] {'seq'}, dimensions={0} | all-to-all | bytes 524288 | tf_op jit(solution)/shard_map/all_to_all | solution.py:273
  157.2 0.7 copy_bitcast_fusion
Async XLA Ops:
  6.5 51.7 %copy-start = (bf16[1024,3,512]{2,0,1:T(8,128)(2,1)S(1)}, bf16[1024,3,512]{2,0,1:T(8,128)(2,1)}, u32[]{:S(2)}) copy-start(bf16[1024,3,512]{2,0,1:T(8,128)(2,1)} %param.11) | copy-start | bytes 9437188
  6.5 51.7 %all-gather.2.cloned.1.call-start = ((), (), s32[]{:S(2)}) async-start(), calls=%async_computation.2 | async-start | bytes 2621440 | tf_op jit(solution)/shard_map/all_gather | solution.py:264
  8.5 29.4 %collective-permute-start = (bf16[256,1024]{1,0:T(8,128)(2,1)S(1)}, bf16[256,1024]{1,0:T(8,128)(2,1)}, u32[]{:S(2)}, u32[]{:S(2)}) collective-permute-start(bf16[256,1024]{1,0:T(8,128)(2,1)S(1)} %fusion.6), channel_id=1, source_target_pairs={{0,0},{1,4},{2,8},{3,12},{4,1},{5,5},{6,9},{7,13},{8,2},{9,6},{10,... | collective-permute-start | bytes 1572872 | tf_op jit(solution)/shard_map/ppermute | solution.py:263
  64.6 76.1 %all-to-all-start = ((bf16[4,3,1024,128]{3,2,1,0:T(8,128)(2,1)}), bf16[4,3,1024,128]{3,2,1,0:T(8,128)(2,1)}, u32[]{:S(2)}, u32[]{:S(2)}) async-start(bf16[4,3,1024,128]{3,2,1,0:T(8,128)(2,1)} %convert_bitcast_fusion), calls=%async_computation | async-start | bytes 6291456 | tf_op jit(solution)/shard_map/all_to_all | solution.py:267
Sparse Core Ops, SparseCore 0:
  38.1 20.0 all-gather.1

commit v2 on v1

--- a/solution.py
+++ b/solution.py
@@ -248,6 +248,213 @@
     )(partial, short_filter, decay_rate, residue, skip.reshape(1, lanes))
 
 
+MESH = pl.DeviceIdType.MESH
+
+
+def partial_sums(parts, subs, x_ref, w_ref, out_ref, held, outbox, from_below, from_above, acc, x_send, x_recv, box_send, below_recv, above_recv):
+    z = lax.axis_index("seq")
+    ch = lax.axis_index("ch")
+    sub = lax.axis_index("sub")
+    k = ch * subs + sub
+    rows = x_ref.shape[0]
+    half = rows // 2
+    lanes = w_ref.shape[2] // parts
+    above = {"seq": lax.rem(z + 1, parts)}
+    below = {"seq": lax.rem(z + parts - 1, parts)}
+    turned = {"seq": k, "ch": z // subs, "sub": lax.rem(z, subs)}
+    sibling = {"sub": 1 - sub}
+    across = {"ch": 1 - ch}
+    moves = k != z
+
+    barrier = pltpu.get_barrier_semaphore()
+
+    def greet(device):
+        pl.semaphore_signal(barrier, inc=1, device_id=device, device_id_type=MESH)
+
+    greet(sibling)
+    greet(across)
+
+    @pl.when(moves)
+    def _():
+        greet(turned)
+
+    @pl.when(z > 0)
+    def _():
+        greet(below)
+
+    @pl.when(z < parts - 1)
+    def _():
+        greet(above)
+
+    peers = 2 + moves.astype(jnp.int32) + (z > 0).astype(jnp.int32) + (z < parts - 1).astype(jnp.int32)
+    pl.semaphore_wait(barrier, peers)
+
+    def piece(h):
+        return pl.ds(h * half, half)
+
+    def copy_x(kind, h, src, slot, device):
+        return pltpu.make_async_remote_copy(
+            src_ref=src,
+            dst_ref=held.at[slot, piece(h)],
+            send_sem=x_send.at[kind, h],
+            recv_sem=x_recv.at[kind, h],
+            device_id=device,
+            device_id_type=MESH,
+        )
+
+    k_sibling = ch * subs + 1 - sub
+    k_across = (1 - ch) * subs + sub
+    k_far = (1 - ch) * subs + 1 - sub
+
+    @pl.when(moves)
+    def _():
+        for h in range(2):
+            copy_x(0, h, x_ref.at[piece(h)], z, turned).start()
+
+    @pl.when(jnp.logical_not(moves))
+    def _():
+        for h in range(2):
+            pltpu.make_async_copy(x_ref.at[piece(h)], held.at[k, piece(h)], x_recv.at[0, h]).start()
+
+    for h in range(2):
+        @pl.when(moves)
+        def _():
+            copy_x(0, h, x_ref.at[piece(h)], k, turned).wait_recv()
+
+        @pl.when(jnp.logical_not(moves))
+        def _():
+            pltpu.make_async_copy(x_ref.at[piece(h)], held.at[k, piece(h)], x_recv.at[0, h]).wait()
+
+        copy_x(1, h, held.at[k, piece(h)], k, across).start()
+        copy_x(2, h, held.at[k, piece(h)], k, sibling).start()
+    for h in range(2):
+        copy_x(1, h, held.at[k, piece(h)], k_across, across).wait_recv()
+        copy_x(3, h, held.at[k_across, piece(h)], k_across, sibling).start()
+    for h in range(2):
+        copy_x(2, h, held.at[k, piece(h)], k_sibling, sibling).wait_recv()
+        copy_x(3, h, held.at[k_across, piece(h)], k_far, sibling).wait_recv()
+
+    def own(j, h):
+        at = pl.ds(pl.multiple_of(j * lanes, lanes), lanes)
+        columns = jnp.concatenate([w_ref[g, :, at] for g in range(3)], axis=1)
+        acc[...] = jnp.dot(held[h], columns, preferred_element_type=jnp.float32)
+
+    def rising(j, h):
+        return pltpu.make_async_remote_copy(
+            src_ref=outbox.at[j, h],
+            dst_ref=from_below.at[j, h],
+            send_sem=box_send.at[j, h],
+            recv_sem=below_recv.at[j, h],
+            device_id=above,
+            device_id_type=MESH,
+        )
+
+    def falling(j, h):
+        return pltpu.make_async_remote_copy(
+            src_ref=outbox.at[j, h],
+            dst_ref=from_above.at[j, h],
+            send_sem=box_send.at[j, h],
+            recv_sem=above_recv.at[j, h],
+            device_id=below,
+            device_id_type=MESH,
+        )
+
+    def add_below(j, h):
+        @pl.when(z > 0)
+        def _():
+            rising(j, h).wait_recv()
+            acc[...] += from_below[j, h].astype(jnp.float32)
+
+    def add_above(j, h):
+        @pl.when(z < parts - 1)
+        def _():
+            falling(j, h).wait_recv()
+            acc[...] += from_above[j, h].astype(jnp.float32)
+
+    def step(u, _):
+        i = u // parts
+        h = lax.rem(u, parts)
+        up = parts - 1 - i
+
+        @pl.when(up > z)
+        def _():
+            own(up, h)
+            add_below(up, h)
+            outbox[up, h] = acc[...].astype(jnp.bfloat16)
+            rising(up, h).start()
+
+        @pl.when(i < z)
+        def _():
+            own(i, h)
+            add_above(i, h)
+            outbox[i, h] = acc[...].astype(jnp.bfloat16)
+            falling(i, h).start()
+
+        return 0
+
+    lax.fori_loop(0, (parts - 1) * parts, step, 0)
+
+    def last(h, _):
+        own(z, h)
+        add_below(z, h)
+        add_above(z, h)
+        for g in range(3):
+            out_ref[0, g, pl.ds(pl.multiple_of(h * rows, rows), rows), :] = acc[:, g * lanes : (g + 1) * lanes].astype(jnp.bfloat16)
+        return 0
+
+    lax.fori_loop(0, parts, last, 0)
+
+    def drain(u, _):
+        j = u // parts
+        h = lax.rem(u, parts)
+
+        @pl.when(j != z)
+        def _():
+            rising(j, h).wait_send()
+
+        return 0
+
+    lax.fori_loop(0, parts * parts, drain, 0)
+
+    @pl.when(moves)
+    def _():
+        for h in range(2):
+            copy_x(0, h, x_ref.at[piece(h)], z, turned).wait_send()
+
+    for h in range(2):
+        copy_x(1, h, held.at[k, piece(h)], k, across).wait_send()
+        copy_x(2, h, held.at[k, piece(h)], k, sibling).wait_send()
+        copy_x(3, h, held.at[k_across, piece(h)], k_across, sibling).wait_send()
+
+
+def summed(inputs, weight, parts, subs):
+    rows, width = inputs.shape
+    lanes = weight.shape[2] // parts
+    box = (parts, parts, rows, 3 * lanes)
+    dma = pltpu.SemaphoreType.DMA
+    return pl.pallas_call(
+        functools.partial(partial_sums, parts, subs),
+        out_shape=jax.ShapeDtypeStruct((1, 3, rows * parts, lanes), jnp.bfloat16),
+        in_specs=[pl.BlockSpec(memory_space=pltpu.VMEM)] * 2,
+        out_specs=pl.BlockSpec(memory_space=pltpu.VMEM),
+        scratch_shapes=[
+            pltpu.VMEM((parts, rows, width), jnp.bfloat16),
+            pltpu.VMEM(box, jnp.bfloat16),
+            pltpu.VMEM(box, jnp.bfloat16),
+            pltpu.VMEM(box, jnp.bfloat16),
+            pltpu.VMEM((rows, 3 * lanes), jnp.float32),
+            dma((4, 2)),
+            dma((4, 2)),
+            dma((parts, parts)),
+            dma((parts, parts)),
+            dma((parts, parts)),
+        ],
+        compiler_params=pltpu.CompilerParams(
+            collective_id=0, has_side_effects=True, vmem_limit_bytes=48 * 2**20
+        ),
+    )(inputs, weight)
+
+
 def fast_shards(token_ids, residual_in, embedding, in_weight, short_filter, decay_rate, residue, skip):
     tok_rows, width = residual_in.shape
     vocab_size = embedding.shape[0]
@@ -259,12 +466,8 @@
     onehot = (token_ids[:, None] == jnp.arange(vocab_size, dtype=jnp.int32)[None, :]).astype(jnp.bfloat16)
     embedded = jnp.dot(onehot, embedding, preferred_element_type=jnp.float32)
     inputs = (residual_in.astype(jnp.float32) + embedded).astype(jnp.bfloat16)
-    pairs = [(i * seq_parts + j, j * seq_parts + i) for i in range(seq_parts) for j in range(seq_parts)]
-    turned = lax.ppermute(inputs, ("seq", "ch", "sub"), pairs)
-    rows_all = lax.all_gather(turned, ("ch", "sub"), axis=0, tiled=True)
-    weight = in_weight.transpose(1, 0, 2).reshape(3, width, seq_parts, lanes)
-    partial = jnp.einsum("td,gdsc->sgtc", rows_all, weight, preferred_element_type=jnp.float32).astype(jnp.bfloat16)
-    partial = lax.all_to_all(partial, "seq", split_axis=0, concat_axis=0, tiled=True)
+    weight = in_weight.transpose(1, 0, 2)
+    partial = summed(inputs, weight, seq_parts, lax.axis_size("sub"))
 
     def own(x):
         return lax.dynamic_slice_in_dim(x, me * lanes, lanes, axis=x.ndim - 1)
@@ -275,7 +478,7 @@
 
 def fits(mesh):
     seq_parts = mesh.shape["seq"]
-    return seq_parts == mesh.shape["ch"] * mesh.shape["sub"]
+    return mesh.shape["ch"] == 2 and mesh.shape["sub"] == 2 and seq_parts == mesh.shape["ch"] * mesh.shape["sub"]
 
 
 def solution(mesh):

time: 168 us -> 127 us (0.76)
  the two profiles are of different devices: /device:TPU:2 before, /device:TPU:0 now
where the time goes in v2:
time: 127 us
  Pallas kernels  101 us (80%)
  blocking collectives  19.4 us (15%)
  local copies, waits for them, and re-layouts  4.88 us (4%)
  matrix products  1.54 us (1%)
    pallas_call x1, Pallas kernels, summed(): pl.pallas_call(functools.partial(partial_sums, parts, subs), out_shape=ja...  97.4 us
    all_to_all x1, blocking collectives, fast_shards(): return lax.all_to_all(mixed, 'seq', split_axis=0, concat_axis=1, tiled=True)  19.4 us
    pallas_call x1, Pallas kernels, convolved(): pl.pallas_call(functools.partial(mix_and_scan, rows, modes), out_shape=ja...  3.46 us

profile of v2, /device:TPU:0, one launch (start us, length us, event | category | flops | bytes accessed | tf_op | source)
XLA Modules:
  0.0 126.6 jit_solution(5048241834694824473)
XLA Ops:
  0.0 0.0 copy-start
  0.0 0.8 constant_dynamic-slice_fusion.2.taps_ref
  0.8 0.8 dynamic-slice_bitcast_fusion.skip_ref
  1.5 0.0 copy-done
  1.5 1.5 %fusion.x_ref = bf16[256,1024]{1,0:T(8,128)(2,1)S(1)} fusion(bf16[512,1024]{1,0:T(8,128)(2,1)S(1)} %copy-done, bf16[256,1024]{1,0:T(8,128)(2,1)} %param.9, s32[256]{0:T(256)} %param.8), kind=kOutput, calls=%fused_computation.1 | convolution fusion | flops 269352960 | bytes 2098176 | tf_op jit(solution)/shard_map/dot_general | solution.py:467
  3.1 0.0 copy-start.1
  3.1 1.9 %copy-done.1 = bf16[1024,3,512]{2,0,1:T(8,128)(2,1)S(1)} copy-done((bf16[1024,3,512]{2,0,1:T(8,128)(2,1)S(1)}, bf16[1024,3,512]{2,0,1:T(8,128)(2,1)}, u32[]{:S(2)}) %copy-start.1) | copy-done | bytes 3145752
  5.0 97.4 %shard_map.82.part_ref = bf16[1,3,1024,128]{3,2,1,0:T(8,128)(2,1)S(1)} custom-call(bf16[256,1024]{1,0:T(8,128)(2,1)S(1)} %fusion.x_ref, bf16[3,1024,512]{2,1,0:T(8,128)(2,1)S(1)} %bitcast.11), custom_call_target="tpu_custom_call" | custom-call | tf_op jit(solution)/shard_map/pallas_call | solution.py:435
  102.4 0.7 constant_dynamic-slice_fusion
  103.1 3.5 %shard_map.83 = bf16[1024,128]{1,0:T(8,128)(2,1)S(1)} custom-call(bf16[1,3,1024,128]{3,2,1,0:T(8,128)(2,1)S(1)} %shard_map.82.part_ref, f32[3,3,128]{2,1,0:T(4,128)S(1)} %constant_dynamic-slice_fusion.2.taps_ref, f32[16,128]{1,0:T(8,128)S(1)} %get-tuple-element.6.rate_ref, f32[16,128]{1,0:T(8,128)S(1)} %get-tuple-element.5.residue_ref, ...), custom_call_target="tpu_custom_call" | custom-call | tf_op jit(solution)/shard_map/pallas_call | solution.py:236
  106.6 19.4 %all_to_all.19 = bf16[4,256,128]{2,1,0:T(8,128)(2,1)S(1)} all-to-all(bf16[4,256,128]{2,1,0:T(8,128)(2,1)S(1)} %bitcast.12), channel_id=1, replica_groups=mesh['grp'=2,'seq'=4,'ch'=2,'sub'=2] {'seq'}, dimensions={0} | all-to-all | bytes 524288 | tf_op jit(solution)/shard_map/all_to_all | solution.py:476
  125.9 0.7 copy_bitcast_fusion
Async XLA Ops:
  0.0 1.5 %copy-start = (bf16[512,1024]{1,0:T(8,128)(2,1)S(1)}, bf16[512,1024]{1,0:T(8,128)(2,1)}, u32[]{:S(2)}) copy-start(bf16[512,1024]{1,0:T(8,128)(2,1)} %param.10) | copy-start | bytes 3145732
  3.1 1.9 %copy-start.1 = (bf16[1024,3,512]{2,0,1:T(8,128)(2,1)S(1)}, bf16[1024,3,512]{2,0,1:T(8,128)(2,1)}, u32[]{:S(2)}) copy-start(bf16[1024,3,512]{2,0,1:T(8,128)(2,1)} %param.11) | copy-start | bytes 9437188

commit v3 on v2

--- a/solution.py
+++ b/solution.py
@@ -165,6 +165,9 @@
 def mix_and_scan(rows, modes, part_ref, taps_ref, rate_ref, residue_ref, skip_ref, out_ref, proj, values, gate, result):
     total, lanes = out_ref.shape
     lead = proj.shape[1] - total
+    at = pl.ds(pl.multiple_of(lax.axis_index("seq") * lanes, lanes), lanes)
+    rates = rate_ref[:, at]
+    weights = residue_ref[:, at]
     taps_count = taps_ref.shape[0]
     span = total // rows
     for g in range(3):
@@ -182,7 +185,7 @@
     for g in range(3):
         acc = None
         for i in range(taps_count):
-            term = taps_ref[i, g : g + 1, :] * proj[g, pl.ds(lead - i, total), :]
+            term = taps_ref[i, g : g + 1, at] * proj[g, pl.ds(lead - i, total), :]
             acc = term if acc is None else acc + term
         if g == 0:
             gate[...] = acc
@@ -190,7 +193,7 @@
             mixed.append(acc)
     values[...] = (mixed[0] * mixed[1]).astype(jnp.bfloat16).astype(jnp.float32)
 
-    decay = [jnp.broadcast_to(jnp.exp(-rate_ref[m : m + 1, :]), (rows, lanes)) for m in range(modes)]
+    decay = [jnp.broadcast_to(jnp.exp(-rates[m : m + 1, :]), (rows, lanes)) for m in range(modes)]
     zero = jnp.zeros((rows, lanes), jnp.float32)
 
     def ends(j, state):
@@ -208,20 +211,20 @@
         carry = down(state[m], 1)
         by = 1
         while by < rows:
-            carry = carry + jnp.exp(-rate_ref[m : m + 1, :] * (span * by)) * down(carry, by)
+            carry = carry + jnp.exp(-rates[m : m + 1, :] * (span * by)) * down(carry, by)
             by *= 2
         entering.append(carry)
-    weight = [jnp.broadcast_to(residue_ref[m : m + 1, :], (rows, lanes)) for m in range(modes)]
-    direct = jnp.broadcast_to(skip_ref[...], (rows, lanes))
+    weight = [jnp.broadcast_to(weights[m : m + 1, :], (rows, lanes)) for m in range(modes)]
+    direct = jnp.broadcast_to(skip_ref[:, at], (rows, lanes))
 
     def scan(j, state):
-        at = pl.ds(j, rows, stride=span)
-        now = values[at, :]
+        here = pl.ds(j, rows, stride=span)
+        now = values[here, :]
         state = tuple(u * d + now for u, d in zip(state, decay))
         terms = [u * w for u, w in zip(state, weight)] + [direct * now]
         while len(terms) > 1:
             terms = [a + b for a, b in zip(terms[::2], terms[1::2])] + terms[len(terms) // 2 * 2 :]
-        result[at, :] = gate[at, :] * terms[0]
+        result[here, :] = gate[here, :] * terms[0]
         return state
 
     lax.fori_loop(0, span, scan, tuple(entering), unroll=4)
@@ -245,7 +248,7 @@
             pltpu.VMEM((total, lanes), f32),
         ],
         compiler_params=pltpu.CompilerParams(vmem_limit_bytes=40 * 2**20),
-    )(partial, short_filter, decay_rate, residue, skip.reshape(1, lanes))
+    )(partial, short_filter, decay_rate, residue, skip.reshape(1, -1))
 
 
 MESH = pl.DeviceIdType.MESH
@@ -257,11 +260,14 @@
     sub = lax.axis_index("sub")
     k = ch * subs + sub
     rows = x_ref.shape[0]
-    half = rows // 2
+    pieces = 4
+    half = rows // pieces
     lanes = w_ref.shape[2] // parts
     above = {"seq": lax.rem(z + 1, parts)}
     below = {"seq": lax.rem(z + parts - 1, parts)}
     turned = {"seq": k, "ch": z // subs, "sub": lax.rem(z, subs)}
+    mirrored = {"seq": k, "ch": 1 - z // subs, "sub": lax.rem(z, subs)}
+    source = {"seq": (1 - ch) * subs + sub, "ch": z // subs, "sub": lax.rem(z, subs)}
     sibling = {"sub": 1 - sub}
     across = {"ch": 1 - ch}
     moves = k != z
@@ -273,6 +279,8 @@
 
     greet(sibling)
     greet(across)
+    greet(mirrored)
+    greet(source)
 
     @pl.when(moves)
     def _():
@@ -286,7 +294,7 @@
     def _():
         greet(above)
 
-    peers = 2 + moves.astype(jnp.int32) + (z > 0).astype(jnp.int32) + (z < parts - 1).astype(jnp.int32)
+    peers = 4 + moves.astype(jnp.int32) + (z > 0).astype(jnp.int32) + (z < parts - 1).astype(jnp.int32)
     pl.semaphore_wait(barrier, peers)
 
     def piece(h):
@@ -305,34 +313,43 @@
     k_sibling = ch * subs + 1 - sub
     k_across = (1 - ch) * subs + sub
     k_far = (1 - ch) * subs + 1 - sub
+    slots = [(k, k_across, k_sibling, k_far), (k_across, k, k_far, k_sibling)]
 
     @pl.when(moves)
     def _():
-        for h in range(2):
+        for h in range(0, pieces, 2):
             copy_x(0, h, x_ref.at[piece(h)], z, turned).start()
 
     @pl.when(jnp.logical_not(moves))
     def _():
-        for h in range(2):
+        for h in range(0, pieces, 2):
             pltpu.make_async_copy(x_ref.at[piece(h)], held.at[k, piece(h)], x_recv.at[0, h]).start()
 
-    for h in range(2):
-        @pl.when(moves)
-        def _():
-            copy_x(0, h, x_ref.at[piece(h)], k, turned).wait_recv()
-
-        @pl.when(jnp.logical_not(moves))
-        def _():
-            pltpu.make_async_copy(x_ref.at[piece(h)], held.at[k, piece(h)], x_recv.at[0, h]).wait()
-
-        copy_x(1, h, held.at[k, piece(h)], k, across).start()
-        copy_x(2, h, held.at[k, piece(h)], k, sibling).start()
-    for h in range(2):
-        copy_x(1, h, held.at[k, piece(h)], k_across, across).wait_recv()
-        copy_x(3, h, held.at[k_across, piece(h)], k_across, sibling).start()
-    for h in range(2):
-        copy_x(2, h, held.at[k, piece(h)], k_sibling, sibling).wait_recv()
-        copy_x(3, h, held.at[k_across, piece(h)], k_far, sibling).wait_recv()
+    for h in range(1, pieces, 2):
+        copy_x(0, h, x_ref.at[piece(h)], z, mirrored).start()
+
+    for h in range(pieces):
+        mine = slots[h % 2][0]
+        if h % 2:
+            copy_x(0, h, x_ref.at[piece(h)], mine, mirrored).wait_recv()
+        else:
+            @pl.when(moves)
+            def _():
+                copy_x(0, h, x_ref.at[piece(h)], mine, turned).wait_recv()
+
+            @pl.when(jnp.logical_not(moves))
+            def _():
+                pltpu.make_async_copy(x_ref.at[piece(h)], held.at[mine, piece(h)], x_recv.at[0, h]).wait()
+
+        copy_x(1, h, held.at[mine, piece(h)], mine, across).start()
+        copy_x(2, h, held.at[mine, piece(h)], mine, sibling).start()
+    for h in range(pieces):
+        other = slots[h % 2][1]
+        copy_x(1, h, held.at[other, piece(h)], other, across).wait_recv()
+        copy_x(3, h, held.at[other, piece(h)], other, sibling).start()
+    for h in range(pieces):
+        copy_x(2, h, held.at[k, piece(h)], slots[h % 2][2], sibling).wait_recv()
+        copy_x(3, h, held.at[k, piece(h)], slots[h % 2][3], sibling).wait_recv()
 
     def own(j, h):
         at = pl.ds(pl.multiple_of(j * lanes, lanes), lanes)
@@ -418,13 +435,14 @@
 
     @pl.when(moves)
     def _():
-        for h in range(2):
+        for h in range(0, pieces, 2):
             copy_x(0, h, x_ref.at[piece(h)], z, turned).wait_send()
 
-    for h in range(2):
-        copy_x(1, h, held.at[k, piece(h)], k, across).wait_send()
-        copy_x(2, h, held.at[k, piece(h)], k, sibling).wait_send()
-        copy_x(3, h, held.at[k_across, piece(h)], k_across, sibling).wait_send()
+    for h in range(1, pieces, 2):
+        copy_x(0, h, x_ref.at[piece(h)], z, mirrored).wait_send()
+    for h in range(pieces):
+        for kind in (1, 2, 3):
+            copy_x(kind, h, held.at[k, piece(h)], k, sibling).wait_send()
 
 
 def summed(inputs, weight, parts, subs):
@@ -443,8 +461,8 @@
             pltpu.VMEM(box, jnp.bfloat16),
             pltpu.VMEM(box, jnp.bfloat16),
             pltpu.VMEM((rows, 3 * lanes), jnp.float32),
-            dma((4, 2)),
-            dma((4, 2)),
+            dma((4, 4)),
+            dma((4, 4)),
             dma((parts, parts)),
             dma((parts, parts)),
             dma((parts, parts)),
@@ -460,19 +478,13 @@
     vocab_size = embedding.shape[0]
     channels = skip.shape[0]
     seq_parts = lax.axis_size("seq")
-    me = lax.axis_index("seq")
-    lanes = channels // seq_parts
-    total = tok_rows * seq_parts
     onehot = (token_ids[:, None] == jnp.arange(vocab_size, dtype=jnp.int32)[None, :]).astype(jnp.bfloat16)
     embedded = jnp.dot(onehot, embedding, preferred_element_type=jnp.float32)
     inputs = (residual_in.astype(jnp.float32) + embedded).astype(jnp.bfloat16)
     weight = in_weight.transpose(1, 0, 2)
     partial = summed(inputs, weight, seq_parts, lax.axis_size("sub"))
 
-    def own(x):
-        return lax.dynamic_slice_in_dim(x, me * lanes, lanes, axis=x.ndim - 1)
-
-    mixed = convolved(partial, own(short_filter), own(decay_rate), own(residue), own(skip))
+    mixed = convolved(partial, short_filter, decay_rate, residue, skip)
     return lax.all_to_all(mixed, "seq", split_axis=0, concat_axis=1, tiled=True)
 
 

time: 127 us -> 122 us (0.961)
  the two profiles are of different devices: /device:TPU:0 before, /device:TPU:2 now
where the time goes in v3:
time: 122 us
  Pallas kernels  97.1 us (80%)
  blocking collectives  19 us (16%)
  local copies, waits for them, and re-layouts  3.84 us (3%)
  matrix products  1.55 us (1%)
    pallas_call x1, Pallas kernels, summed(): pl.pallas_call(functools.partial(partial_sums, parts, subs), out_shape=ja...  93.7 us
    all_to_all x1, blocking collectives, fast_shards(): return lax.all_to_all(mixed, 'seq', split_axis=0, concat_axis=1, tiled=True)  19 us
    pallas_call x1, Pallas kernels, convolved(): pl.pallas_call(functools.partial(mix_and_scan, rows, modes), out_shape=ja...  3.39 us
    unnamed x12, local copies, waits for them, and re-layouts  3.11 us

profile of v3, /device:TPU:2, one launch (start us, length us, event | category | flops | bytes accessed | tf_op | source)
XLA Modules:
  0.0 121.6 jit_solution(529074406856807068)
XLA Ops:
  0.0 0.0 copy-start
  0.0 0.0 copy-start.5
  0.0 0.0 copy-start.3
  0.0 0.0 copy-start.2
  0.0 1.2 copy-done
  1.2 0.0 copy-start.4
  1.2 1.5 %fusion.x_ref = bf16[256,1024]{1,0:T(8,128)(2,1)S(1)} fusion(bf16[512,1024]{1,0:T(8,128)(2,1)S(1)} %copy-done, bf16[256,1024]{1,0:T(8,128)(2,1)} %param.9, s32[256]{0:T(256)} %param.8), kind=kOutput, calls=%fused_computation.1 | convolution fusion | flops 269352960 | bytes 2098176 | tf_op jit(solution)/shard_map/dot_general | solution.py:482
  2.8 0.0 copy-start.1
  2.8 1.9 %copy-done.1 = bf16[1024,3,512]{2,0,1:T(8,128)(2,1)S(1)} copy-done((bf16[1024,3,512]{2,0,1:T(8,128)(2,1)S(1)}, bf16[1024,3,512]{2,0,1:T(8,128)(2,1)}, u32[]{:S(2)}) %copy-start.1) | copy-done | bytes 3145752
  4.7 93.7 %shard_map.82.part_ref = bf16[1,3,1024,128]{3,2,1,0:T(8,128)(2,1)S(1)} custom-call(bf16[256,1024]{1,0:T(8,128)(2,1)S(1)} %fusion.x_ref, bf16[3,1024,512]{2,1,0:T(8,128)(2,1)S(1)} %bitcast.10), custom_call_target="tpu_custom_call" | custom-call | tf_op jit(solution)/shard_map/pallas_call | solution.py:453
  98.4 0.0 copy-done.5
  98.4 0.0 copy-done.3
  98.4 0.0 copy-done.2
  98.4 0.0 copy-done.4
  98.5 3.4 %shard_map.83 = bf16[1024,128]{1,0:T(8,128)(2,1)S(1)} custom-call(bf16[1,3,1024,128]{3,2,1,0:T(8,128)(2,1)S(1)} %shard_map.82.part_ref, f32[3,3,512]{2,1,0:T(4,128)S(1)} %copy-done.4, f32[16,512]{1,0:T(8,128)S(1)} %copy-done.2, f32[16,512]{1,0:T(8,128)S(1)} %copy-done.3, f32[1,512]{1,0:T(1,128)S(1)} %bitcast.12), custom_call_target="tpu_custom_call" | custom-call | tf_op jit(solution)/shard_map/pallas_call | solution.py:239
  101.9 19.0 %all_to_all.19 = bf16[4,256,128]{2,1,0:T(8,128)(2,1)S(1)} all-to-all(bf16[4,256,128]{2,1,0:T(8,128)(2,1)S(1)} %bitcast.11), channel_id=1, replica_groups=mesh['grp'=2,'seq'=4,'ch'=2,'sub'=2] {'seq'}, dimensions={0} | all-to-all | bytes 524288 | tf_op jit(solution)/shard_map/all_to_all | solution.py:488
  120.8 0.7 copy_bitcast_fusion
Async XLA Ops:
  0.0 1.2 %copy-start = (bf16[512,1024]{1,0:T(8,128)(2,1)S(1)}, bf16[512,1024]{1,0:T(8,128)(2,1)}, u32[]{:S(2)}) copy-start(bf16[512,1024]{1,0:T(8,128)(2,1)} %param.10) | copy-start | bytes 3145732
  0.0 98.4 %copy-start.5 = (f32[512]{0:T(512)S(1)}, f32[512]{0:T(512)}, u32[]{:S(2)}) copy-start(f32[512]{0:T(512)} %param.15) | copy-start | bytes 6148
  0.0 98.4 %copy-start.3 = (f32[16,512]{1,0:T(8,128)S(1)}, f32[16,512]{1,0:T(8,128)}, u32[]{:S(2)}) copy-start(f32[16,512]{1,0:T(8,128)} %residue_ref.1) | copy-start | bytes 98308
  0.0 98.4 %copy-start.2 = (f32[16,512]{1,0:T(8,128)S(1)}, f32[16,512]{1,0:T(8,128)}, u32[]{:S(2)}) copy-start(f32[16,512]{1,0:T(8,128)} %rate_ref.1) | copy-start | bytes 98308
  1.2 97.2 %copy-start.4 = (f32[3,3,512]{2,1,0:T(4,128)S(1)}, f32[3,3,512]{2,1,0:T(4,128)}, u32[]{:S(2)}) copy-start(f32[3,3,512]{2,1,0:T(4,128)} %taps_ref.1) | copy-start | bytes 55300
  2.8 1.9 %copy-start.1 = (bf16[1024,3,512]{2,0,1:T(8,128)(2,1)S(1)}, bf16[1024,3,512]{2,0,1:T(8,128)(2,1)}, u32[]{:S(2)}) copy-start(bf16[1024,3,512]{2,0,1:T(8,128)(2,1)} %param.11) | copy-start | bytes 9437188

commit v4 on v3

--- a/solution.py
+++ b/solution.py
@@ -347,9 +347,8 @@
         other = slots[h % 2][1]
         copy_x(1, h, held.at[other, piece(h)], other, across).wait_recv()
         copy_x(3, h, held.at[other, piece(h)], other, sibling).start()
-    for h in range(pieces):
-        copy_x(2, h, held.at[k, piece(h)], slots[h % 2][2], sibling).wait_recv()
-        copy_x(3, h, held.at[k, piece(h)], slots[h % 2][3], sibling).wait_recv()
+    def block_at(q):
+        return lax.rem(ch + q, 2) * subs + lax.rem(sub + q // 2, 2)
 
     def own(j, h):
         at = pl.ds(pl.multiple_of(j * lanes, lanes), lanes)
@@ -390,8 +389,14 @@
 
     def step(u, _):
         i = u // parts
-        h = lax.rem(u, parts)
+        h = block_at(lax.rem(u, parts))
         up = parts - 1 - i
+
+        @pl.when(u == 2)
+        def _():
+            for n in range(pieces):
+                copy_x(2, n, held.at[k, piece(n)], slots[n % 2][2], sibling).wait_recv()
+                copy_x(3, n, held.at[k, piece(n)], slots[n % 2][3], sibling).wait_recv()
 
         @pl.when(up > z)
         def _():
@@ -411,7 +416,8 @@
 
     lax.fori_loop(0, (parts - 1) * parts, step, 0)
 
-    def last(h, _):
+    def last(q, _):
+        h = block_at(q)
         own(z, h)
         add_below(z, h)
         add_above(z, h)

time: 122 us -> 117 us (0.959)
  Pallas kernels: 97.1 us -> 92.1 us
    pallas_call x1, Pallas kernels: 93.7 us -> 88.7 us  [summed(): pl.pallas_call(functools.partial(partial_sums, parts, subs), out_shape=ja...]
where the time goes in v4:
time: 117 us; the launch traced here: 116 us
  Pallas kernels  92.1 us (79%)
  blocking collectives  18.7 us (16%)
  local copies, waits for them, and re-layouts  3.84 us (3%)
  matrix products  1.55 us (1%)
    pallas_call x1, Pallas kernels, summed(): pl.pallas_call(functools.partial(partial_sums, parts, subs), out_shape=ja...  88.7 us
    all_to_all x1, blocking collectives, fast_shards(): return lax.all_to_all(mixed, 'seq', split_axis=0, concat_axis=1, tiled=True)  18.7 us
    pallas_call x1, Pallas kernels, convolved(): pl.pallas_call(functools.partial(mix_and_scan, rows, modes), out_shape=ja...  3.39 us
    unnamed x12, local copies, waits for them, and re-layouts  3.11 us

profile of v4, /device:TPU:2, one launch (start us, length us, event | category | flops | bytes accessed | tf_op | source)
XLA Modules:
  0.0 116.3 jit_solution(15610011629520209739)
XLA Ops:
  0.0 0.0 copy-start
  0.0 0.0 copy-start.5
  0.0 0.0 copy-start.3
  0.0 0.0 copy-start.2
  0.0 1.2 %copy-done = bf16[512,1024]{1,0:T(8,128)(2,1)S(1)} copy-done((bf16[512,1024]{1,0:T(8,128)(2,1)S(1)}, bf16[512,1024]{1,0:T(8,128)(2,1)}, u32[]{:S(2)}) %copy-start) | copy-done | bytes 1048600
  1.2 0.0 copy-start.4
  1.2 1.5 %fusion.x_ref = bf16[256,1024]{1,0:T(8,128)(2,1)S(1)} fusion(bf16[512,1024]{1,0:T(8,128)(2,1)S(1)} %copy-done, bf16[256,1024]{1,0:T(8,128)(2,1)} %param.9, s32[256]{0:T(256)} %param.8), kind=kOutput, calls=%fused_computation.1 | convolution fusion | flops 269352960 | bytes 2098176 | tf_op jit(solution)/shard_map/dot_general | solution.py:488
  2.8 0.0 copy-start.1
  2.8 1.9 %copy-done.1 = bf16[1024,3,512]{2,0,1:T(8,128)(2,1)S(1)} copy-done((bf16[1024,3,512]{2,0,1:T(8,128)(2,1)S(1)}, bf16[1024,3,512]{2,0,1:T(8,128)(2,1)}, u32[]{:S(2)}) %copy-start.1) | copy-done | bytes 3145752
  4.7 88.7 %shard_map.82.part_ref = bf16[1,3,1024,128]{3,2,1,0:T(8,128)(2,1)S(1)} custom-call(bf16[256,1024]{1,0:T(8,128)(2,1)S(1)} %fusion.x_ref, bf16[3,1024,512]{2,1,0:T(8,128)(2,1)S(1)} %bitcast.10), custom_call_target="tpu_custom_call" | custom-call | tf_op jit(solution)/shard_map/pallas_call | solution.py:459
  93.4 0.0 copy-done.5
  93.4 0.0 copy-done.3
  93.4 0.0 copy-done.2
  93.4 0.0 copy-done.4
  93.5 3.4 %shard_map.83 = bf16[1024,128]{1,0:T(8,128)(2,1)S(1)} custom-call(bf16[1,3,1024,128]{3,2,1,0:T(8,128)(2,1)S(1)} %shard_map.82.part_ref, f32[3,3,512]{2,1,0:T(4,128)S(1)} %copy-done.4, f32[16,512]{1,0:T(8,128)S(1)} %copy-done.2, f32[16,512]{1,0:T(8,128)S(1)} %copy-done.3, f32[1,512]{1,0:T(1,128)S(1)} %bitcast.12), custom_call_target="tpu_custom_call" | custom-call | tf_op jit(solution)/shard_map/pallas_call | solution.py:239
  96.9 18.7 %all_to_all.19 = bf16[4,256,128]{2,1,0:T(8,128)(2,1)S(1)} all-to-all(bf16[4,256,128]{2,1,0:T(8,128)(2,1)S(1)} %bitcast.11), channel_id=1, replica_groups=mesh['grp'=2,'seq'=4,'ch'=2,'sub'=2] {'seq'}, dimensions={0} | all-to-all | bytes 524288 | tf_op jit(solution)/shard_map/all_to_all | solution.py:494
  115.6 0.7 copy_bitcast_fusion
Async XLA Ops:
  0.0 1.2 %copy-start = (bf16[512,1024]{1,0:T(8,128)(2,1)S(1)}, bf16[512,1024]{1,0:T(8,128)(2,1)}, u32[]{:S(2)}) copy-start(bf16[512,1024]{1,0:T(8,128)(2,1)} %param.10) | copy-start | bytes 3145732
  0.0 93.4 %copy-start.5 = (f32[512]{0:T(512)S(1)}, f32[512]{0:T(512)}, u32[]{:S(2)}) copy-start(f32[512]{0:T(512)} %param.15) | copy-start | bytes 6148
  0.0 93.4 %copy-start.3 = (f32[16,512]{1,0:T(8,128)S(1)}, f32[16,512]{1,0:T(8,128)}, u32[]{:S(2)}) copy-start(f32[16,512]{1,0:T(8,128)} %residue_ref.1) | copy-start | bytes 98308
  0.0 93.4 %copy-start.2 = (f32[16,512]{1,0:T(8,128)S(1)}, f32[16,512]{1,0:T(8,128)}, u32[]{:S(2)}) copy-start(f32[16,512]{1,0:T(8,128)} %rate_ref.1) | copy-start | bytes 98308
  1.2 92.2 %copy-start.4 = (f32[3,3,512]{2,1,0:T(4,128)S(1)}, f32[3,3,512]{2,1,0:T(4,128)}, u32[]{:S(2)}) copy-start(f32[3,3,512]{2,1,0:T(4,128)} %taps_ref.1) | copy-start | bytes 55300
  2.8 1.9 %copy-start.1 = (bf16[1024,3,512]{2,0,1:T(8,128)(2,1)S(1)}, bf16[1024,3,512]{2,0,1:T(8,128)(2,1)}, u32[]{:S(2)}) copy-start(bf16[1024,3,512]{2,0,1:T(8,128)(2,1)} %param.11) | copy-start | bytes 9437188

commit v5 on v4

--- a/solution.py
+++ b/solution.py
@@ -260,7 +260,7 @@
     sub = lax.axis_index("sub")
     k = ch * subs + sub
     rows = x_ref.shape[0]
-    pieces = 4
+    pieces = 8
     half = rows // pieces
     lanes = w_ref.shape[2] // parts
     above = {"seq": lax.rem(z + 1, parts)}
@@ -395,8 +395,12 @@
         @pl.when(u == 2)
         def _():
             for n in range(pieces):
-                copy_x(2, n, held.at[k, piece(n)], slots[n % 2][2], sibling).wait_recv()
-                copy_x(3, n, held.at[k, piece(n)], slots[n % 2][3], sibling).wait_recv()
+                copy_x(2 + n % 2, n, held.at[k, piece(n)], k_sibling, sibling).wait_recv()
+
+        @pl.when(u == 3)
+        def _():
+            for n in range(pieces):
+                copy_x(3 - n % 2, n, held.at[k, piece(n)], k_far, sibling).wait_recv()
 
         @pl.when(up > z)
         def _():
@@ -467,8 +471,8 @@
             pltpu.VMEM(box, jnp.bfloat16),
             pltpu.VMEM(box, jnp.bfloat16),
             pltpu.VMEM((rows, 3 * lanes), jnp.float32),
-            dma((4, 4)),
-            dma((4, 4)),
+            dma((4, 8)),
+            dma((4, 8)),
             dma((parts, parts)),
             dma((parts, parts)),
             dma((parts, parts)),

time: 117 us -> 116 us (level)
  no operation moved by 1% of the time
where the time goes in v5:
time: 116 us
  Pallas kernels  92.1 us (79%)
  blocking collectives  18.7 us (16%)
  local copies, waits for them, and re-layouts  3.84 us (3%)
  matrix products  1.55 us (1%)
    pallas_call x1, Pallas kernels, summed(): pl.pallas_call(functools.partial(partial_sums, parts, subs), out_shape=ja...  88.7 us
    all_to_all x1, blocking collectives, fast_shards(): return lax.all_to_all(mixed, 'seq', split_axis=0, concat_axis=1, tiled=True)  18.7 us
    pallas_call x1, Pallas kernels, convolved(): pl.pallas_call(functools.partial(mix_and_scan, rows, modes), out_shape=ja...  3.39 us
    unnamed x12, local copies, waits for them, and re-layouts  3.11 us

profile of v5, /device:TPU:2, one launch (start us, length us, event | category | flops | bytes accessed | tf_op | source)
XLA Modules:
  0.0 116.2 jit_solution(2400003824295741581)
XLA Ops:
  0.0 0.0 copy-start
  0.0 0.0 copy-start.5
  0.0 0.0 copy-start.3
  0.0 0.0 copy-start.2
  0.0 1.2 %copy-done = bf16[512,1024]{1,0:T(8,128)(2,1)S(1)} copy-done((bf16[512,1024]{1,0:T(8,128)(2,1)S(1)}, bf16[512,1024]{1,0:T(8,128)(2,1)}, u32[]{:S(2)}) %copy-start) | copy-done | bytes 1048600
  1.2 0.0 copy-start.4
  1.2 1.5 %fusion.x_ref = bf16[256,1024]{1,0:T(8,128)(2,1)S(1)} fusion(bf16[512,1024]{1,0:T(8,128)(2,1)S(1)} %copy-done, bf16[256,1024]{1,0:T(8,128)(2,1)} %param.9, s32[256]{0:T(256)} %param.8), kind=kOutput, calls=%fused_computation.1 | convolution fusion | flops 269352960 | bytes 2098176 | tf_op jit(solution)/shard_map/dot_general | solution.py:492
  2.8 0.0 copy-start.1
  2.8 1.9 %copy-done.1 = bf16[1024,3,512]{2,0,1:T(8,128)(2,1)S(1)} copy-done((bf16[1024,3,512]{2,0,1:T(8,128)(2,1)S(1)}, bf16[1024,3,512]{2,0,1:T(8,128)(2,1)}, u32[]{:S(2)}) %copy-start.1) | copy-done | bytes 3145752
  4.7 88.7 %shard_map.82.part_ref = bf16[1,3,1024,128]{3,2,1,0:T(8,128)(2,1)S(1)} custom-call(bf16[256,1024]{1,0:T(8,128)(2,1)S(1)} %fusion.x_ref, bf16[3,1024,512]{2,1,0:T(8,128)(2,1)S(1)} %bitcast.10), custom_call_target="tpu_custom_call" | custom-call | tf_op jit(solution)/shard_map/pallas_call | solution.py:463
  93.4 0.0 copy-done.5
  93.4 0.0 copy-done.3
  93.4 0.0 copy-done.2
  93.4 0.0 copy-done.4
  93.4 3.4 %shard_map.83 = bf16[1024,128]{1,0:T(8,128)(2,1)S(1)} custom-call(bf16[1,3,1024,128]{3,2,1,0:T(8,128)(2,1)S(1)} %shard_map.82.part_ref, f32[3,3,512]{2,1,0:T(4,128)S(1)} %copy-done.4, f32[16,512]{1,0:T(8,128)S(1)} %copy-done.2, f32[16,512]{1,0:T(8,128)S(1)} %copy-done.3, f32[1,512]{1,0:T(1,128)S(1)} %bitcast.12), custom_call_target="tpu_custom_call" | custom-call | tf_op jit(solution)/shard_map/pallas_call | solution.py:239
  96.8 18.7 %all_to_all.19 = bf16[4,256,128]{2,1,0:T(8,128)(2,1)S(1)} all-to-all(bf16[4,256,128]{2,1,0:T(8,128)(2,1)S(1)} %bitcast.11), channel_id=1, replica_groups=mesh['grp'=2,'seq'=4,'ch'=2,'sub'=2] {'seq'}, dimensions={0} | all-to-all | bytes 524288 | tf_op jit(solution)/shard_map/all_to_all | solution.py:498
  115.5 0.7 copy_bitcast_fusion
Async XLA Ops:
  0.0 1.2 %copy-start = (bf16[512,1024]{1,0:T(8,128)(2,1)S(1)}, bf16[512,1024]{1,0:T(8,128)(2,1)}, u32[]{:S(2)}) copy-start(bf16[512,1024]{1,0:T(8,128)(2,1)} %param.10) | copy-start | bytes 3145732
  0.0 93.4 %copy-start.5 = (f32[512]{0:T(512)S(1)}, f32[512]{0:T(512)}, u32[]{:S(2)}) copy-start(f32[512]{0:T(512)} %param.15) | copy-start | bytes 6148
  0.0 93.4 %copy-start.3 = (f32[16,512]{1,0:T(8,128)S(1)}, f32[16,512]{1,0:T(8,128)}, u32[]{:S(2)}) copy-start(f32[16,512]{1,0:T(8,128)} %residue_ref.1) | copy-start | bytes 98308
  0.0 93.4 %copy-start.2 = (f32[16,512]{1,0:T(8,128)S(1)}, f32[16,512]{1,0:T(8,128)}, u32[]{:S(2)}) copy-start(f32[16,512]{1,0:T(8,128)} %rate_ref.1) | copy-start | bytes 98308
  1.2 92.2 %copy-start.4 = (f32[3,3,512]{2,1,0:T(4,128)S(1)}, f32[3,3,512]{2,1,0:T(4,128)}, u32[]{:S(2)}) copy-start(f32[3,3,512]{2,1,0:T(4,128)} %taps_ref.1) | copy-start | bytes 55300
  2.8 1.9 %copy-start.1 = (bf16[1024,3,512]{2,0,1:T(8,128)(2,1)S(1)}, bf16[1024,3,512]{2,0,1:T(8,128)(2,1)}, u32[]{:S(2)}) copy-start(bf16[1024,3,512]{2,0,1:T(8,128)(2,1)} %param.11) | copy-start | bytes 9437188
